TPU v7x, 32 devices: a whole 2x2x4 slice. The times are simulated.
32 devices in a mesh: row: 8 (over y, x, core), col: 4 (over z).
Axes of the slice: x: 2, y: 2, z: 4, core: 2. Of those that a mesh axis runs over, the one named last changes fastest.
Arguments:
- matrix: float32 [10240, 10240], P('row', 'col'), may hold values from 0 to 1.5, as said below
Outputs:
- factored: float32 [10240, 10240], P('row', 'col')
Inputs may be any that keep to these rules, and one draw needn't show every extreme that they name: A Gaussian kernel matrix over random embeddings plus a ridge on the diagonal, stored block-cyclically; symmetric positive definite, diagonal entries near 1.5.
All inputs are finite; a program needn't handle non-finite values.
Results may differ from a plain program's by a relative error of at most 0.0003.
Values sent between devices are 32-bit elements; how exact they have to be, the bound alone decides.
A program may use at most 192 MiB of HBM per device.

v0:
```python
import jax
import jax.numpy as jnp
from jax import lax
from jax.sharding import PartitionSpec as P

NB = 256


def spread(array, axis, root):
    mine = lax.axis_index(axis) == root
    return lax.psum(jnp.where(mine, array, jnp.zeros_like(array)), axis)


def make_panel(col_block, k, row_tiles):
    tiles_here = col_block.shape[0] // NB
    diag_block = spread(col_block[:NB], "row", k)
    factor_low = jnp.linalg.cholesky(diag_block)
    inverse = lax.linalg.triangular_solve(
        factor_low, jnp.eye(NB, dtype=factor_low.dtype), left_side=True, lower=True
    )
    scaled = jnp.dot(col_block, inverse.T, precision=lax.Precision.HIGHEST)
    tile_copy = jnp.tile(factor_low, (tiles_here, 1))
    marks = row_tiles[:, None]
    row_panel = jnp.where(marks > k, scaled, jnp.where(marks == k, tile_copy, 0.0))
    return spread(row_panel, "col", k)


def column_panel(row_panel):
    tiles_here = row_panel.shape[0] // NB
    n_row = lax.axis_size("row")
    n_col = lax.axis_size("col")
    groups = n_row // n_col
    pieces = [spread(row_panel, "row", lax.axis_index("col") + m * n_col) for m in range(groups)]
    chosen = jnp.stack(pieces).reshape(groups, tiles_here, NB, NB)
    return chosen.transpose(1, 0, 2, 3).reshape(tiles_here * groups * NB, NB)


def local(matrix):
    local_rows, local_cols = matrix.shape
    n_row = lax.axis_size("row")
    n_col = lax.axis_size("col")
    row_index = lax.axis_index("row")
    col_index = lax.axis_index("col")
    row_tiles = jnp.arange(local_rows, dtype=jnp.int32) // NB * n_row + row_index
    col_tiles = jnp.arange(local_cols, dtype=jnp.int32) // NB * n_col + col_index
    highest = lax.Precision.HIGHEST
    panel_first = make_panel(matrix[:, :NB], 0, row_tiles)
    across_first = column_panel(panel_first)
    rows_first = panel_first * (row_tiles > 0)[:, None]
    cols_first = across_first * (col_tiles > 0)[:, None]
    current = matrix - jnp.dot(rows_first, cols_first.T, precision=highest)
    panel_second = make_panel(current[:, :NB], 1, row_tiles)
    across_second = column_panel(panel_second)
    rows_second = panel_second * (row_tiles > 1)[:, None]
    cols_second = across_second * (col_tiles > 1)[:, None]
    current = current - jnp.dot(rows_second, cols_second.T, precision=highest)
    lead_cols = current[:, :NB]
    lead_cols = jnp.where(col_index == 0, panel_first, lead_cols)
    lead_cols = jnp.where(col_index == 1, panel_second, lead_cols)
    current = current.at[:, :NB].set(lead_cols)
    zero_mask = (row_tiles[:, None] == 0) & (col_tiles[None, :] > 0) | (row_tiles[:, None] == 1) & (
        col_tiles[None, :] > 1
    )
    return jnp.where(zero_mask, 0.0, current)


def solution(mesh):
    placed = (P("row", "col"),)
    return jax.shard_map(
        local, mesh=mesh, in_specs=placed, out_specs=P("row", "col"), check_vma=False
    )
```

profile of v0, /device:TPU:25, one launch (start us, length us, event | category | flops | bytes accessed | tf_op | source)
XLA Modules:
  0.0 597.9 jit_solution(3242503386733762147)
XLA Ops:
  6.5 13.9 %copy.18 = f32[1280,2560]{0,1:T(8,128)} copy(f32[1280,2560]{1,0:T(8,128)} %param.6) | data formatting | bytes 26214400 | tf_op args[0]
  20.4 1.7 slice_select_fusion.1
  22.2 54.1 %all-reduce.10.cloned.1.call-done = f32[256,256]{0,1:T(8,128)} async-done(((f32[256,256]{0,1:T(8,128)}), f32[256,256]{0,1:T(8,128)}) %all-reduce.10.cloned.1.call-update) | async-done | bytes 262160 | tf_op jit(solution)/shard_map/psum | solution.py:11
  76.3 1.1 copy.13
  77.4 1.0 fusion.16
  78.4 11.7 %cholesky.130 = f32[128,128]{1,0:T(8,128)S(1)} custom-call(f32[128,128]{1,0:T(8,128)S(1)} %cholesky.194), custom_call_target="Cholesky" | custom-call | tf_op jit(solution)/shard_map/jit(cholesky)/cholesky | solution.py:17
  90.1 9.8 %custom-call.13 = f32[1,128,128]{1,2,0:T(8,128)S(1)} custom-call(f32[1,128,128]{2,1,0:T(8,128)S(1)} %get-tuple-element.74), custom_call_target="InvertDiagBlocksLowerTriangular" | custom-call | tf_op jit(solution)/shard_map/jit(cholesky)/cholesky | solution.py:17
  100.4 11.7 %cholesky.147 = f32[128,128]{1,0:T(8,128)S(1)} custom-call(f32[128,128]{1,0:T(8,128)S(1)} %convolution_subtract_fusion.5), custom_call_target="Cholesky" | custom-call | tf_op jit(solution)/shard_map/jit(cholesky)/cholesky | solution.py:17
  112.2 0.7 compare_reduce_fusion.2
  114.3 4.2 while.5
  115.2 1.3 bitcast_dynamic-update-slice_fusion.4
  117.2 1.3 bitcast_dynamic-update-slice_fusion.4
  118.6 19.7 %custom-call.14 = f32[2,128,128]{1,2,0:T(8,128)S(1)} custom-call(f32[2,128,128]{2,1,0:T(8,128)S(1)} %get-tuple-element.33), custom_call_target="InvertDiagBlocksLowerTriangular" | custom-call | tf_op jit(solution)/shard_map/triangular_solve/custom-call.0 | solution.py:18
  139.7 3.7 fusion.2
  143.4 58.9 %all-reduce.12.cloned.1.call-done = f32[1280,256]{0,1:T(8,128)} async-done(((f32[1280,256]{0,1:T(8,128)}), f32[1280,256]{0,1:T(8,128)}) %all-reduce.12.cloned.1.call-update) | async-done | bytes 1310736 | tf_op jit(solution)/shard_map/psum | solution.py:11
  202.4 1.5 broadcast_select_fusion.2
  203.9 1.5 copy.15
  205.4 1.5 copy.16
  207.0 65.0 %all-reduce.20.cloned.1.call-done = (f32[1,5,256,256]{3,2,1,0:T(8,128)}, f32[1,5,256,256]{3,2,1,0:T(8,128)}) async-done(((f32[1,5,256,256]{3,2,1,0:T(8,128)}, f32[1,5,256,256]{3,2,1,0:T(8,128)}), (f32[1,5,256,256]{3,2,1,0:T(8,128)}, f32[1,5,256,256]{3,2,1,0:T(8,128)})) %all-reduce.20.cloned.1.call-update) | async-done | bytes 2621456 | tf_op jit(solution)/shard_map/psum | solution.py:11
  272.0 2.0 maximum_bitcast_fusion
  274.6 0.9 copy-done.1
  275.5 15.0 %convolution_subtract_fusion.1 = f32[1280,2560]{0,1:T(8,128)S(1)} fusion(f32[1280,2560]{0,1:T(8,128)} %copy.18, f32[2560,256]{1,0:T(8,128)S(1)} %bitcast_multiply_fusion.1, f32[1280,256]{0,1:T(8,128)S(1)} %copy-done.1, f32[1280]{0:T(1024)S(1)} %fusion.53), kind=kOutput, calls=%fused_computation.5 | convolution fusion | flops 10069934080 | bytes 30151680 | tf_op jit(solution)/shard_map/dot_general | solution.py:51
  290.5 4.9 copy-done
  296.5 53.2 %all-reduce.14.cloned.1.call-done = f32[256,256]{0,1:T(8,128)} async-done(((f32[256,256]{0,1:T(8,128)}), f32[256,256]{0,1:T(8,128)}) %all-reduce.14.cloned.1.call-update) | async-done | bytes 262160 | tf_op jit(solution)/shard_map/psum | solution.py:11
  349.7 1.1 copy.20
  350.8 1.0 fusion.15
  351.8 11.7 %cholesky.164 = f32[128,128]{1,0:T(8,128)S(1)} custom-call(f32[128,128]{1,0:T(8,128)S(1)} %cholesky.197), custom_call_target="Cholesky" | custom-call | tf_op jit(solution)/shard_map/jit(cholesky)/cholesky | solution.py:17
  363.6 9.8 %custom-call.15 = f32[1,128,128]{1,2,0:T(8,128)S(1)} custom-call(f32[1,128,128]{2,1,0:T(8,128)S(1)} %get-tuple-element.70), custom_call_target="InvertDiagBlocksLowerTriangular" | custom-call | tf_op jit(solution)/shard_map/jit(cholesky)/cholesky | solution.py:17
  373.9 11.7 %cholesky.181 = f32[128,128]{1,0:T(8,128)S(1)} custom-call(f32[128,128]{1,0:T(8,128)S(1)} %convolution_subtract_fusion.4), custom_call_target="Cholesky" | custom-call | tf_op jit(solution)/shard_map/jit(cholesky)/cholesky | solution.py:17
  388.3 4.3 while.6
  389.3 1.3 bitcast_dynamic-update-slice_fusion.5
  391.3 1.3 bitcast_dynamic-update-slice_fusion.5
  392.7 19.7 %custom-call.16 = f32[2,128,128]{1,2,0:T(8,128)S(1)} custom-call(f32[2,128,128]{2,1,0:T(8,128)S(1)} %get-tuple-element.34), custom_call_target="InvertDiagBlocksLowerTriangular" | custom-call | tf_op jit(solution)/shard_map/triangular_solve/custom-call.0 | solution.py:18
  413.2 1.2 tile.20
  414.4 1.7 copy.21
  416.1 3.7 fusion
  420.0 58.9 %all-reduce.16.cloned.1.call-done = f32[1280,256]{0,1:T(8,128)} async-done(((f32[1280,256]{0,1:T(8,128)}), f32[1280,256]{0,1:T(8,128)}) %all-reduce.16.cloned.1.call-update) | async-done | bytes 1310736 | tf_op jit(solution)/shard_map/psum | solution.py:11
  478.9 2.6 broadcast_select_fusion.3
  481.5 2.8 copy.23
  484.3 1.5 copy.24
  485.8 1.0 compare_reduce_fusion.4
  486.8 64.1 %all-reduce.18.cloned.1.call-done = (f32[1,5,256,256]{3,2,1,0:T(8,128)}, f32[1,5,256,256]{3,2,1,0:T(8,128)}) async-done(((f32[1,5,256,256]{3,2,1,0:T(8,128)}, f32[1,5,256,256]{3,2,1,0:T(8,128)}), (f32[1,5,256,256]{3,2,1,0:T(8,128)}, f32[1,5,256,256]{3,2,1,0:T(8,128)})) %all-reduce.18.cloned.1.call-update) | async-done | bytes 2621456 | tf_op jit(solution)/shard_map/psum | solution.py:11
  550.9 2.0 maximum_bitcast_fusion.1
  553.5 0.9 copy-done.2
  554.4 15.0 %convolution_subtract_fusion = f32[1280,2560]{0,1:T(8,128)S(1)} fusion(f32[1280,2560]{0,1:T(8,128)} %copy-done, f32[2560,256]{1,0:T(8,128)S(1)} %bitcast_multiply_fusion, f32[1280,256]{0,1:T(8,128)S(1)} %copy-done.2, f32[1280]{0:T(1024)S(1)} %fusion.54), kind=kOutput, calls=%fused_computation.4 | convolution fusion | flops 10069934080 | bytes 30151680 | tf_op jit(solution)/shard_map/dot_general | solution.py:56
  569.4 1.3 select_dynamic-update-slice_fusion
  570.7 5.9 or_select_fusion
  576.6 13.9 %copy.27 = f32[1280,2560]{1,0:T(8,128)} copy(f32[1280,2560]{0,1:T(8,128)} %or_select_fusion) | data formatting | bytes 26214400 | tf_op jit(solution)/shard_map/jit(_where)/select_n | solution.py:64
  (64 shorter events, 10.1 us)
Async XLA Ops:
  6.5 69.8 %all-reduce.10.cloned.1.call-start = ((), (), s32[]{:S(2)}) async-start(), calls=%async_computation | async-start | bytes 524288 | tf_op jit(solution)/shard_map/psum | solution.py:11
  22.1 180.3 %all-reduce.12.cloned.1.call-start = ((), (), s32[]{:S(2)}) async-start(), calls=%async_computation.1 | async-start | bytes 2621440 | tf_op jit(solution)/shard_map/psum | solution.py:11
  143.4 128.6 %all-reduce.20.cloned.1.call-start = ((), (), s32[]{:S(2)}) async-start(), calls=%async_computation.5 | async-start | bytes 5242880 | tf_op jit(solution)/shard_map/psum | solution.py:11
  206.9 142.9 %all-reduce.14.cloned.1.call-start = ((), (), s32[]{:S(2)}) async-start(), calls=%async_computation.2 | async-start | bytes 524288 | tf_op jit(solution)/shard_map/psum | solution.py:11
  274.2 1.3 copy-start.1
  290.5 5.0 copy-start
  296.2 182.7 %all-reduce.16.cloned.1.call-start = ((), (), s32[]{:S(2)}) async-start(), calls=%async_computation.3 | async-start | bytes 2621440 | tf_op jit(solution)/shard_map/psum | solution.py:11
  419.9 131.0 %all-reduce.18.cloned.1.call-start = ((), (), s32[]{:S(2)}) async-start(), calls=%async_computation.4 | async-start | bytes 5242880 | tf_op jit(solution)/shard_map/psum | solution.py:11
  553.1 1.3 copy-start.2
Sparse Core Ops, SparseCore 0:
  22.2 53.9 all-reduce.9
  143.5 58.8 all-reduce.11
  207.0 64.9 all-reduce.19
  296.3 53.3 all-reduce.13
  420.0 58.8 all-reduce.15
  485.9 64.9 all-reduce.17
where the time goes:
time: 610 us; the launch traced here: 598 us
  waiting for transfers between devices  354 us (58%)
  other arithmetic  130 us (21%)
  local copies, waits for them, and re-layouts  55.9 us (9%)
  matrix products  40.2 us (7%)
  between operations  16.9 us (3%)
    psum x6, waiting for transfers between devices, spread(): return lax.psum(jnp.where(mine, array, jnp.zeros_like(array)), axis)  354 us
    another operation x13, other arithmetic, make_panel(): factor_low = jnp.linalg.cholesky(diag_block)  68.7 us
    another operation x5, other arithmetic, make_panel(): lax.linalg.triangular_solve(factor_low, jnp.eye(NB, dtype=factor_low.dtyp...  39.4 us
    unnamed x7, local copies, waits for them, and re-layouts  20.6 us
    dot_general x1, matrix products, local(): current = matrix - jnp.dot(rows_first, cols_first.T, precision=highest)  15 us
    dot_general x1, matrix products, local(): current = current - jnp.dot(rows_second, cols_second.T, precision=highest)  15 us
    select_n x1, local copies, waits for them, and re-layouts, local(): return jnp.where(zero_mask, 0.0, current)  13.9 us
  transfers between devices with their start and end apart: 6, of which 6 were waited for; matrix products, arithmetic and copies ran while one was open for 0% of the time, Pallas kernels for 0%

commit v1 on v0

v1 whole, which is shorter than its diff:
```python
import functools
import jax
import jax.numpy as jnp
from jax import lax
from jax.experimental import pallas as pl
from jax.experimental.pallas import tpu as pltpu
from jax.sharding import PartitionSpec as P

NB = 256
BK = 32
MESH = pl.DeviceIdType.MESH
HIGH = lax.Precision.HIGHEST


def dot(a, b, dims=((1,), (0,))):
    return lax.dot_general(a, b, (dims, ((), ())), precision=HIGH, preferred_element_type=jnp.float32)


def factor_block(work, lt_ref, v_ref, k):
    base = pl.multiple_of(k * BK, BK)
    rows = work[pl.ds(base, BK), :]
    lead = pltpu.roll(rows[:, :NB], lax.rem(NB - base, NB), 1)[:, :128]
    lane = lax.broadcasted_iota(jnp.int32, (BK, 128), 1)
    sub = lax.broadcasted_iota(jnp.int32, (BK, 128), 0)
    w = jnp.where(lane < BK, lead, jnp.where(lane == sub + BK, 1.0, 0.0))
    scale = jnp.ones((BK, 128), jnp.float32)
    for j in range(0, BK, 2):
        c0 = jnp.broadcast_to(w[:, j:j + 1], (BK, 128))
        c1 = jnp.broadcast_to(w[:, j + 1:j + 2], (BK, 128))
        r0 = jnp.broadcast_to(w[j:j + 1, :], (BK, 128))
        r1 = jnp.broadcast_to(w[j + 1:j + 2, :], (BK, 128))
        d = jnp.broadcast_to(c0[j:j + 1, :], (BK, 128))
        e = jnp.broadcast_to(c0[j + 1:j + 2, :], (BK, 128))
        f = jnp.broadcast_to(c1[j + 1:j + 2, :], (BK, 128))
        inv_d = 1.0 / d
        inv_f = d / (f * d - e * e)
        ratio = e * inv_d
        m0 = jnp.where(sub > j, c0 * inv_d, 0.0)
        r1n = r1 - ratio * r0
        m1 = jnp.where(sub > j + 1, (c1 - ratio * c0) * inv_f, 0.0)
        w = w - m0 * r0 - m1 * r1n
        scale = jnp.where(sub == j, inv_d, jnp.where(sub == j + 1, inv_f, scale))
    w = w * jnp.sqrt(scale)
    vd = pltpu.roll(w, 128 - BK, 1)[:, :BK]
    new = dot(vd, rows)
    wide = lax.broadcasted_iota(jnp.int32, (BK, NB), 1)
    tall = lax.broadcasted_iota(jnp.int32, (BK, NB), 0)
    top = jnp.where(wide >= tall + base, new[:, :NB], 0.0)
    lt_ref[pl.ds(base, BK), :] = top
    v_ref[pl.ds(base, BK), :] = new[:, NB:]
    left = jnp.where(wide >= base + BK, top, 0.0)
    right = jnp.concatenate([top, new[:, NB:]], axis=1)
    work[...] = work[...] - dot(left, right, ((0,), (0,)))


def set_work(work, tile):
    work[:, :NB] = tile
    a = lax.broadcasted_iota(jnp.int32, (NB, NB), 0)
    b = lax.broadcasted_iota(jnp.int32, (NB, NB), 1)
    work[:, NB:] = jnp.where(a == b, 1.0, 0.0)


def pick(index, table):
    out = jnp.int32(0)
    for i, value in enumerate(table):
        out = out + jnp.where(index == i, jnp.int32(value), jnp.int32(0))
    return out


def chain_kernel(n_row, n_col, chunks, a_ref, r_out, c_out, v_out, lt_out, mid_out,
                 rbuf, cbuf, dbuf, work, r_send, r_recv, c_send, c_recv, d_send, d_recv, loc):
    row = lax.axis_index("row")
    col = lax.axis_index("col")
    n_rows = rbuf.shape[1]
    n_cols = cbuf.shape[2]
    r_step = n_rows // chunks
    c_step = n_cols // chunks
    half = n_row // 2
    order = [i ^ (i >> 1) for i in range(half)]
    orders = [order, order[:1] + order[:0:-1]]
    pair = row // 2
    core = lax.rem(row, 2)
    sibling = row + 1 - 2 * core
    nexts, hops, lasts = [], [], []
    for k in range(2):
        table = [0] * half
        where = [0] * half
        for i, q in enumerate(orders[k]):
            table[q] = orders[k][(i + 1) % half]
            where[q] = i
        nexts.append(2 * pick(pair, table) + k)
        place = pick(pair, where)
        hops.append(jnp.where(core == k, place, place + 1))
        lasts.append(place == half - 1)

    def remote(src, ssem, rsem, target):
        return pltpu.make_async_remote_copy(
            src_ref=src, dst_ref=src, send_sem=ssem, recv_sem=rsem, device_id=target, device_id_type=MESH)

    def local(src, dst, sem):
        return pltpu.make_async_copy(src, dst, sem)

    own = []
    for k in range(2):
        own.append((col == k, local(a_ref.at[:, pl.ds(0, NB)], rbuf.at[k], loc.at[2 * k])))
        own.append((row == k, local(a_ref.at[pl.ds(0, NB), :], cbuf.at[k], loc.at[2 * k + 1])))
    roots = ((0, 0), (1, 0), (1, 1))
    for i, (a, b) in enumerate(roots):
        own.append(((row == a) & (col == b), local(a_ref.at[pl.ds(0, NB), pl.ds(0, NB)], dbuf.at[i], loc.at[4 + i])))
    for cond, copy in own:
        pl.when(cond)(copy.start)

    barrier = pltpu.get_barrier_semaphore()
    for i in range(1, n_row):
        pl.semaphore_signal(barrier, inc=1, device_id=(lax.rem(row + i, n_row), col), device_id_type=MESH)
    for i in range(1, n_col):
        pl.semaphore_signal(barrier, inc=1, device_id=(row, lax.rem(col + i, n_col)), device_id_type=MESH)
    pl.semaphore_wait(barrier, n_row + n_col - 2)
    for cond, copy in own:
        pl.when(cond)(copy.wait)

    d_sends = []
    for i, (a, b) in enumerate(roots):
        tile = dbuf.at[i]
        k = a
        root = (row == a) & (col == b)
        recv = remote(tile, d_send.at[i, 0], d_recv.at[i], (row, col))
        pl.when(jnp.logical_not(root))(recv.wait_recv)
        up = (row == a) & (col >= b) & (col < n_col - 1)
        down = (row == a) & (col <= b) & (col > 0)
        sends = (
            (up, remote(tile, d_send.at[i, 0], d_recv.at[i], (row, jnp.minimum(col + 1, n_col - 1)))),
            (down, remote(tile, d_send.at[i, 1], d_recv.at[i], (row, jnp.maximum(col - 1, 0)))),
            ((core == k) & jnp.logical_not(lasts[k]), remote(tile, d_send.at[i, 2], d_recv.at[i], (nexts[k], col))),
            (core == k, remote(tile, d_send.at[i, 3], d_recv.at[i], (sibling, col))),
        )
        for cond, copy in sends:
            pl.when(cond)(copy.start)
        d_sends.extend(sends)

    def r_piece(k, c):
        return rbuf.at[k, pl.ds(pl.multiple_of(c * r_step, r_step), r_step), :]

    def c_piece(k, c):
        return cbuf.at[k, :, pl.ds(pl.multiple_of(c * c_step, c_step), c_step)]

    def r_sends(k, c):
        piece = r_piece(k, c)
        return (
            ((col >= k) & (col < n_col - 1),
             remote(piece, r_send.at[k, 0, c], r_recv.at[k, c], (row, jnp.minimum(col + 1, n_col - 1)))),
            ((col <= k) & (col > 0),
             remote(piece, r_send.at[k, 1, c], r_recv.at[k, c], (row, jnp.maximum(col - 1, 0)))),
        )

    def c_sends(k, c):
        piece = c_piece(k, c)
        return (
            ((core == k) & jnp.logical_not(lasts[k]),
             remote(piece, c_send.at[k, 0, c], c_recv.at[k, c], (nexts[k], col))),
            (core == k, remote(piece, c_send.at[k, 1, c], c_recv.at[k, c], (sibling, col))),
        )

    def pump(s):
        for k in range(2):
            far = jnp.where(col >= k, col - k, k - col)

            def r_one(c, k=k, far=far):
                pl.when(far > 0)(remote(r_piece(k, c), r_send.at[k, 0, c], r_recv.at[k, c], (row, col)).wait_recv)
                for cond, copy in r_sends(k, c):
                    pl.when(cond)(copy.start)

            def c_one(c, k=k):
                pl.when(row != k)(remote(c_piece(k, c), c_send.at[k, 0, c], c_recv.at[k, c], (row, col)).wait_recv)
                for cond, copy in c_sends(k, c):
                    pl.when(cond)(copy.start)

            pl.when((s >= far) & (s < far + chunks))(lambda: r_one(s - far))
            hop = hops[k]
            pl.when((s >= hop) & (s < hop + chunks))(lambda: c_one(s - hop))

    blocks = NB // BK
    set_work(work, dbuf[0])

    def first(s, carry):
        pump(s)
        factor_block(work, lt_out.at[0], v_out.at[0], s)
        return carry

    lax.fori_loop(0, blocks, first, 0)
    mid = dot(dbuf[1], v_out[0], ((1,), (1,)))
    mid_out[...] = mid
    set_work(work, dbuf[2] - dot(mid, mid, ((1,), (1,))))

    def second(s, carry):
        pump(s + blocks)
        factor_block(work, lt_out.at[1], v_out.at[1], s)
        return carry

    lax.fori_loop(0, blocks, second, 0)

    total = chunks + max(n_col, half + 1)
    if total > 2 * blocks:
        def rest(s, carry):
            pump(s)
            return carry

        lax.fori_loop(2 * blocks, total, rest, 0)

    back = [local(rbuf, r_out, loc.at[0]), local(cbuf, c_out, loc.at[1])]
    for copy in back:
        copy.start()
    for cond, copy in d_sends:
        pl.when(cond)(copy.wait_send)

    def drain(c, carry):
        for k in range(2):
            for cond, copy in r_sends(k, c) + c_sends(k, c):
                pl.when(cond)(copy.wait_send)
        return carry

    lax.fori_loop(0, chunks, drain, 0)
    for copy in back:
        copy.wait()


def halves(x):
    hi = x.astype(jnp.bfloat16)
    lo = (x - hi.astype(jnp.float32)).astype(jnp.bfloat16)
    return hi, lo


def update_kernel(n_row, n_col, a_ref, r_ref, c_ref, v_ref, lt_ref, mid_ref, o_ref, right):
    t = pl.program_id(0)
    row = lax.axis_index("row")
    col = lax.axis_index("col")
    n_cols = a_ref.shape[1]

    @pl.when(t == 0)
    def _():
        @pl.loop(0, n_cols // NB)
        def _(s):
            span = pl.ds(pl.multiple_of(s * NB, NB), NB)
            p0 = dot(v_ref[0], c_ref[0, :, span])
            p1 = dot(v_ref[1], c_ref[1, :, span] - dot(mid_ref[...], p0))
            for k, p in enumerate((p0, p1)):
                hi, lo = halves(p)
                right[pl.ds(3 * k * NB, NB), span] = hi
                right[pl.ds((3 * k + 1) * NB, NB), span] = lo
                right[pl.ds((3 * k + 2) * NB, NB), span] = hi

    g = t * n_row + row
    q0 = dot(r_ref[0], v_ref[0], ((1,), (1,)))
    q1 = dot(r_ref[1] - dot(q0, mid_ref[...], ((1,), (1,))), v_ref[1], ((1,), (1,)))
    h0, l0 = halves(q0)
    h1, l1 = halves(q1)
    left = jnp.concatenate([h0, h0, l0, h1, h1, l1], axis=1)
    wide = 2 * NB if n_cols % (2 * NB) == 0 else NB

    @pl.loop(0, n_cols // wide)
    def _(s):
        span = pl.ds(pl.multiple_of(s * wide, wide), wide)
        o_ref[:, span] = a_ref[:, span] - lax.dot_general(
            left, right[:, span], (((1,), (0,)), ((), ())), preferred_element_type=jnp.float32)

    @pl.when(g < 2)
    def _():
        o_ref[...] = jnp.zeros_like(o_ref)

    @pl.when(col == 0)
    def _():
        o_ref[:, :NB] = q0

        @pl.when(g == 0)
        def _():
            o_ref[:, :NB] = lt_ref[0].T

    @pl.when((col == 1) & (g > 0))
    def _():
        o_ref[:, :NB] = q1

        @pl.when(g == 1)
        def _():
            o_ref[:, :NB] = lt_ref[1].T


def body(n_row, n_col, matrix):
    n_rows, n_cols = matrix.shape
    chunks = 10
    f32 = jnp.float32
    anyspace = pl.BlockSpec(memory_space=pl.ANY)
    vmem = pl.BlockSpec(memory_space=pltpu.VMEM)
    r, c, v, lt, mid = pl.pallas_call(
        functools.partial(chain_kernel, n_row, n_col, chunks),
        out_shape=(
            jax.ShapeDtypeStruct((2, n_rows, NB), f32),
            jax.ShapeDtypeStruct((2, NB, n_cols), f32),
            jax.ShapeDtypeStruct((2, NB, NB), f32),
            jax.ShapeDtypeStruct((2, NB, NB), f32),
            jax.ShapeDtypeStruct((NB, NB), f32),
        ),
        in_specs=[anyspace],
        out_specs=(anyspace, anyspace, vmem, vmem, vmem),
        scratch_shapes=[
            pltpu.VMEM((2, n_rows, NB), f32),
            pltpu.VMEM((2, NB, n_cols), f32),
            pltpu.VMEM((3, NB, NB), f32),
            pltpu.VMEM((NB, 2 * NB), f32),
            pltpu.SemaphoreType.DMA((2, 2, chunks)),
            pltpu.SemaphoreType.DMA((2, chunks)),
            pltpu.SemaphoreType.DMA((2, 2, chunks)),
            pltpu.SemaphoreType.DMA((2, chunks)),
            pltpu.SemaphoreType.DMA((3, 4)),
            pltpu.SemaphoreType.DMA((3,)),
            pltpu.SemaphoreType.DMA((7,)),
        ],
        compiler_params=pltpu.CompilerParams(
            collective_id=0, has_side_effects=True, vmem_limit_bytes=24 * 2**20),
        name="chain",
    )(matrix)
    whole = lambda shape: pl.BlockSpec(shape, lambda t: (0,) * len(shape), pipeline_mode=pl.Buffered(1))
    return pl.pallas_call(
        functools.partial(update_kernel, n_row, n_col),
        grid=(n_rows // NB,),
        out_shape=jax.ShapeDtypeStruct(matrix.shape, f32),
        in_specs=[
            pl.BlockSpec((NB, n_cols), lambda t: (t, 0)),
            pl.BlockSpec((2, NB, NB), lambda t: (0, t, 0)),
            whole((2, NB, n_cols)),
            whole((2, NB, NB)),
            whole((2, NB, NB)),
            whole((NB, NB)),
        ],
        out_specs=pl.BlockSpec((NB, n_cols), lambda t: (t, 0)),
        scratch_shapes=[pltpu.VMEM((6 * NB, n_cols), jnp.bfloat16)],
        compiler_params=pltpu.CompilerParams(vmem_limit_bytes=48 * 2**20),
        name="update",
    )(matrix, r, c, v, lt, mid)


def solution(mesh):
    n_row, n_col = mesh.shape["row"], mesh.shape["col"]
    return jax.shard_map(
        functools.partial(body, n_row, n_col), mesh=mesh,
        in_specs=(P("row", "col"),), out_specs=P("row", "col"), check_vma=False)
```

time: 610 us -> 172 us (0.28)
  the two profiles are of different devices: /device:TPU:25 before, /device:TPU:26 now
where the time goes in v1:
time: 172 us; the launch traced here: 171 us
  Pallas kernels  164 us (95%)
  local copies, waits for them, and re-layouts  7.01 us (4%)
    pallas_call x1, Pallas kernels, body(): pl.pallas_call(functools.partial(chain_kernel, n_row, n_col, chunks), out...  124 us
    pallas_call x1, Pallas kernels, body(): pl.pallas_call(functools.partial(update_kernel, n_row, n_col), grid=(n_ro...  40.7 us
    unnamed x4, local copies, waits for them, and re-layouts  7.01 us

profile of v1, /device:TPU:26, one launch (start us, length us, event | category | flops | bytes accessed | tf_op | source)
XLA Modules:
  0.0 171.4 jit_solution(1371285674565707721)
XLA Ops:
  0.0 0.0 copy-start
  0.0 4.7 %copy-done = f32[1280,2560]{1,0:T(8,128)S(1)} copy-done((f32[1280,2560]{1,0:T(8,128)S(1)}, f32[1280,2560]{1,0:T(8,128)}, u32[]{:S(2)}) %copy-start) | copy-done | bytes 13107224
  4.7 123.7 %chain.1 = (f32[2,1280,256]{2,1,0:T(8,128)S(1)}, f32[2,256,2560]{2,1,0:T(8,128)S(1)}, f32[2,256,256]{2,1,0:T(8,128)S(1)}, f32[2,256,256]{2,1,0:T(8,128)S(1)}, f32[256,256]{1,0:T(8,128)S(1)}) custom-call(f32[1280,2560]{1,0:T(8,128)S(1)} %copy-done), custom_call_target="tpu_custom_call" | custom-call | tf_op jit(solution)/shard_map/chain/pallas_call | solution.py:293
  128.4 0.0 copy-start.1
  128.4 2.3 %copy-done.1 = f32[2,256,2560]{2,1,0:T(8,128)} copy-done((f32[2,256,2560]{2,1,0:T(8,128)}, f32[2,256,2560]{2,1,0:T(8,128)S(1)}, u32[]{:S(2)}) %copy-start.1) | copy-done | bytes 5242904
  130.7 40.7 %update.1 = f32[1280,2560]{1,0:T(8,128)} custom-call(f32[1280,2560]{1,0:T(8,128)} %a_ref.3, f32[2,1280,256]{2,1,0:T(8,128)S(1)} %get-tuple-element.10.r_ref, f32[2,256,2560]{2,1,0:T(8,128)} %copy-done.1, f32[2,256,256]{2,1,0:T(8,128)S(1)} %get-tuple-element.12.v_ref, f32[2,256,256]{2,1,0:T(8,128)S(1)} %get-tuple-element.13.lt_ref, ...), custom_call_target="tpu_custom_call" | custom-call | tf_op jit(solution)/shard_map/update/pallas_call | solution.py:322
Async XLA Ops:
  0.0 4.7 %copy-start = (f32[1280,2560]{1,0:T(8,128)S(1)}, f32[1280,2560]{1,0:T(8,128)}, u32[]{:S(2)}) copy-start(f32[1280,2560]{1,0:T(8,128)} %a_ref.3) | copy-start | bytes 39321604
  128.4 2.3 %copy-start.1 = (f32[2,256,2560]{2,1,0:T(8,128)}, f32[2,256,2560]{2,1,0:T(8,128)S(1)}, u32[]{:S(2)}) copy-start(f32[2,256,2560]{2,1,0:T(8,128)S(1)} %get-tuple-element.11.c_ref) | copy-start | bytes 15728644

commit v2 on v1

--- a/solution.py
+++ b/solution.py
@@ -8,6 +8,7 @@
 
 NB = 256
 BK = 32
+PIECES = 4
 MESH = pl.DeviceIdType.MESH
 HIGH = lax.Precision.HIGHEST
 
@@ -81,17 +82,22 @@
     pair = row // 2
     core = lax.rem(row, 2)
     sibling = row + 1 - 2 * core
-    nexts, hops, lasts = [], [], []
+    nexts, hops, lasts, prevs, fwd, bwd, ring_hops = [], [], [], [], [], [], []
     for k in range(2):
-        table = [0] * half
-        where = [0] * half
+        table, where, before = [0] * half, [0] * half, [0] * half
         for i, q in enumerate(orders[k]):
             table[q] = orders[k][(i + 1) % half]
+            before[q] = orders[k][(i - 1) % half]
             where[q] = i
+        place = pick(pair, where)
         nexts.append(2 * pick(pair, table) + k)
-        place = pick(pair, where)
+        prevs.append(2 * pick(pair, before) + k)
         hops.append(jnp.where(core == k, place, place + 1))
         lasts.append(place == half - 1)
+        fwd.append((core == k) & (place < half // 2))
+        bwd.append((core == k) & ((place == 0) | (place > half // 2 + 1)))
+        near = jnp.where(place <= half // 2, place, half - place)
+        ring_hops.append(jnp.where(core == k, near, near + 1))
 
     def remote(src, ssem, rsem, target):
         return pltpu.make_async_remote_copy(
@@ -119,24 +125,34 @@
     for cond, copy in own:
         pl.when(cond)(copy.wait)
 
-    d_sends = []
-    for i, (a, b) in enumerate(roots):
-        tile = dbuf.at[i]
+    d_step = NB // PIECES
+
+    def d_sends(i, p):
+        a, b = roots[i]
         k = a
-        root = (row == a) & (col == b)
-        recv = remote(tile, d_send.at[i, 0], d_recv.at[i], (row, col))
-        pl.when(jnp.logical_not(root))(recv.wait_recv)
+        tile = dbuf.at[i, pl.ds(pl.multiple_of(p * d_step, d_step), d_step), :]
         up = (row == a) & (col >= b) & (col < n_col - 1)
         down = (row == a) & (col <= b) & (col > 0)
-        sends = (
-            (up, remote(tile, d_send.at[i, 0], d_recv.at[i], (row, jnp.minimum(col + 1, n_col - 1)))),
-            (down, remote(tile, d_send.at[i, 1], d_recv.at[i], (row, jnp.maximum(col - 1, 0)))),
-            ((core == k) & jnp.logical_not(lasts[k]), remote(tile, d_send.at[i, 2], d_recv.at[i], (nexts[k], col))),
-            (core == k, remote(tile, d_send.at[i, 3], d_recv.at[i], (sibling, col))),
+        return tile, (
+            (up, remote(tile, d_send.at[i, 0, p], d_recv.at[i, p], (row, jnp.minimum(col + 1, n_col - 1)))),
+            (down, remote(tile, d_send.at[i, 1, p], d_recv.at[i, p], (row, jnp.maximum(col - 1, 0)))),
+            (fwd[k], remote(tile, d_send.at[i, 2, p], d_recv.at[i, p], (nexts[k], col))),
+            (bwd[k], remote(tile, d_send.at[i, 3, p], d_recv.at[i, p], (prevs[k], col))),
+            (core == k, remote(tile, d_send.at[i, 4, p], d_recv.at[i, p], (sibling, col))),
         )
-        for cond, copy in sends:
-            pl.when(cond)(copy.start)
-        d_sends.extend(sends)
+
+    def d_relay(i):
+        a, b = roots[i]
+
+        def step(p, carry):
+            tile, sends = d_sends(i, p)
+            pl.when((row != a) | (col != b))(
+                remote(tile, d_send.at[i, 0, p], d_recv.at[i, p], (row, col)).wait_recv)
+            for cond, copy in sends:
+                pl.when(cond)(copy.start)
+            return carry
+
+        lax.fori_loop(0, PIECES, step, 0)
 
     def r_piece(k, c):
         return rbuf.at[k, pl.ds(pl.multiple_of(c * r_step, r_step), r_step), :]
@@ -161,23 +177,59 @@
             (core == k, remote(piece, c_send.at[k, 1, c], c_recv.at[k, c], (sibling, col))),
         )
 
-    def pump(s):
+    early = chunks // 2
+
+    def r_root(k):
+        def step(c, carry):
+            up, down = r_sends(k, c)
+            pl.when((col == k) & up[0] & ((k == 0) | (c < early)))(up[1].start)
+            pl.when((col == k) & down[0])(down[1].start)
+            return carry
+
+        lax.fori_loop(0, chunks, step, 0)
+
+    def c_root(k):
+        def step(c, carry):
+            for cond, copy in c_sends(k, c):
+                pl.when((row == k) & cond)(copy.start)
+            return carry
+
+        lax.fori_loop(0, chunks, step, 0)
+
+    def pump(s, tiles=True):
+        if tiles:
+            for i in (1, 2):
+                pl.when((row != roots[i][0]) & (s == ring_hops[roots[i][0]]))(lambda i=i: d_relay(i))
         for k in range(2):
             far = jnp.where(col >= k, col - k, k - col)
 
-            def r_one(c, k=k, far=far):
-                pl.when(far > 0)(remote(r_piece(k, c), r_send.at[k, 0, c], r_recv.at[k, c], (row, col)).wait_recv)
+            def r_one(c, k=k):
+                pl.when(col != k)(remote(r_piece(k, c), r_send.at[k, 0, c], r_recv.at[k, c], (row, col)).wait_recv)
                 for cond, copy in r_sends(k, c):
-                    pl.when(cond)(copy.start)
+                    pl.when((col != k) & cond)(copy.start)
+                if k == 1:
+                    @pl.when((col == k) & (c < chunks - early))
+                    def _():
+                        cond, copy = r_sends(k, c + early)[0]
+                        pl.when(cond)(copy.start)
 
             def c_one(c, k=k):
-                pl.when(row != k)(remote(c_piece(k, c), c_send.at[k, 0, c], c_recv.at[k, c], (row, col)).wait_recv)
+                remote(c_piece(k, c), c_send.at[k, 0, c], c_recv.at[k, c], (row, col)).wait_recv()
                 for cond, copy in c_sends(k, c):
                     pl.when(cond)(copy.start)
 
-            pl.when((s >= far) & (s < far + chunks))(lambda: r_one(s - far))
+            u = s - far
+            c = (5 * jnp.maximum(u, 0) + 6) // 7
+            pl.when((u >= 0) & ((7 * c) // 5 == u) & (c < chunks))(lambda: r_one(c))
             hop = hops[k]
-            pl.when((s >= hop) & (s < hop + chunks))(lambda: c_one(s - hop))
+            pl.when((s >= hop) & (s < hop + chunks) & (row != k))(lambda: c_one(s - hop))
+
+    pl.when(row > 1)(lambda: [r_root(k) for k in range(2)] and None)
+    d_relay(0)
+    pl.when(row == 1)(lambda: [d_relay(i) for i in (1, 2)] and None)
+    pl.when(row <= 1)(lambda: [r_root(k) for k in range(2)] and None)
+    for k in range(2):
+        pl.when(row == k)(functools.partial(c_root, k))
 
     blocks = NB // BK
     set_work(work, dbuf[0])
@@ -188,21 +240,29 @@
         return carry
 
     lax.fori_loop(0, blocks, first, 0)
+    most = half // 2 + 2
+    if most > blocks:
+        def tiles_rest(s, carry):
+            for i in (1, 2):
+                pl.when((row != roots[i][0]) & (s == ring_hops[roots[i][0]]))(lambda i=i: d_relay(i))
+            return carry
+
+        lax.fori_loop(blocks, most, tiles_rest, 0)
     mid = dot(dbuf[1], v_out[0], ((1,), (1,)))
     mid_out[...] = mid
     set_work(work, dbuf[2] - dot(mid, mid, ((1,), (1,))))
 
     def second(s, carry):
-        pump(s + blocks)
+        pump(s + blocks, False)
         factor_block(work, lt_out.at[1], v_out.at[1], s)
         return carry
 
     lax.fori_loop(0, blocks, second, 0)
 
-    total = chunks + max(n_col, half + 1)
+    total = max((7 * (chunks - 1)) // 5 + n_col, chunks + half)
     if total > 2 * blocks:
         def rest(s, carry):
-            pump(s)
+            pump(s, False)
             return carry
 
         lax.fori_loop(2 * blocks, total, rest, 0)
@@ -210,8 +270,14 @@
     back = [local(rbuf, r_out, loc.at[0]), local(cbuf, c_out, loc.at[1])]
     for copy in back:
         copy.start()
-    for cond, copy in d_sends:
-        pl.when(cond)(copy.wait_send)
+
+    def d_drain(p, carry):
+        for i in range(3):
+            for cond, copy in d_sends(i, p)[1]:
+                pl.when(cond)(copy.wait_send)
+        return carry
+
+    lax.fori_loop(0, PIECES, d_drain, 0)
 
     def drain(c, carry):
         for k in range(2):
@@ -230,6 +296,11 @@
     return hi, lo
 
 
+def dot3(a, b, dims=((1,), (0,))):
+    part = lambda x, y: lax.dot_general(x, y, (dims, ((), ())), preferred_element_type=jnp.float32)
+    return part(a[0], b[0]) + (part(a[0], b[1]) + part(a[1], b[0]))
+
+
 def update_kernel(n_row, n_col, a_ref, r_ref, c_ref, v_ref, lt_ref, mid_ref, o_ref, right):
     t = pl.program_id(0)
     row = lax.axis_index("row")
@@ -241,18 +312,20 @@
         @pl.loop(0, n_cols // NB)
         def _(s):
             span = pl.ds(pl.multiple_of(s * NB, NB), NB)
-            p0 = dot(v_ref[0], c_ref[0, :, span])
-            p1 = dot(v_ref[1], c_ref[1, :, span] - dot(mid_ref[...], p0))
-            for k, p in enumerate((p0, p1)):
-                hi, lo = halves(p)
+            p0 = halves(dot3(halves(v_ref[0]), halves(c_ref[0, :, span])))
+            rest = c_ref[1, :, span] - dot3(halves(mid_ref[...]), p0)
+            p1 = halves(dot3(halves(v_ref[1]), halves(rest)))
+            for k, (hi, lo) in enumerate((p0, p1)):
                 right[pl.ds(3 * k * NB, NB), span] = hi
                 right[pl.ds((3 * k + 1) * NB, NB), span] = lo
                 right[pl.ds((3 * k + 2) * NB, NB), span] = hi
 
     g = t * n_row + row
-    q0 = dot(r_ref[0], v_ref[0], ((1,), (1,)))
-    q1 = dot(r_ref[1] - dot(q0, mid_ref[...], ((1,), (1,))), v_ref[1], ((1,), (1,)))
+    across = ((1,), (1,))
+    q0 = dot3(halves(r_ref[0]), halves(v_ref[0]), across)
     h0, l0 = halves(q0)
+    rest = r_ref[1] - dot3((h0, l0), halves(mid_ref[...]), across)
+    q1 = dot3(halves(rest), halves(v_ref[1]), across)
     h1, l1 = halves(q1)
     left = jnp.concatenate([h0, h0, l0, h1, h1, l1], axis=1)
     wide = 2 * NB if n_cols % (2 * NB) == 0 else NB
@@ -310,12 +383,12 @@
             pltpu.SemaphoreType.DMA((2, chunks)),
             pltpu.SemaphoreType.DMA((2, 2, chunks)),
             pltpu.SemaphoreType.DMA((2, chunks)),
-            pltpu.SemaphoreType.DMA((3, 4)),
-            pltpu.SemaphoreType.DMA((3,)),
+            pltpu.SemaphoreType.DMA((3, 5, PIECES)),
+            pltpu.SemaphoreType.DMA((3, PIECES)),
             pltpu.SemaphoreType.DMA((7,)),
         ],
         compiler_params=pltpu.CompilerParams(
-            collective_id=0, has_side_effects=True, vmem_limit_bytes=24 * 2**20),
+            collective_id=0, has_side_effects=True, vmem_limit_bytes=60 * 2**20),
         name="chain",
     )(matrix)
     whole = lambda shape: pl.BlockSpec(shape, lambda t: (0,) * len(shape), pipeline_mode=pl.Buffered(1))
@@ -333,7 +406,7 @@
         ],
         out_specs=pl.BlockSpec((NB, n_cols), lambda t: (t, 0)),
         scratch_shapes=[pltpu.VMEM((6 * NB, n_cols), jnp.bfloat16)],
-        compiler_params=pltpu.CompilerParams(vmem_limit_bytes=48 * 2**20),
+        compiler_params=pltpu.CompilerParams(vmem_limit_bytes=60 * 2**20),
         name="update",
     )(matrix, r, c, v, lt, mid)
 

time: 172 us -> 140 us (0.81)
  the two profiles are of different devices: /device:TPU:26 before, /device:TPU:25 now
where the time goes in v2:
time: 140 us
  Pallas kernels  140 us (100%)
    pallas_call x1, Pallas kernels, body(): pl.pallas_call(functools.partial(chain_kernel, n_row, n_col, chunks), out...  107 us
    pallas_call x1, Pallas kernels, body(): pl.pallas_call(functools.partial(update_kernel, n_row, n_col), grid=(n_ro...  33.5 us

profile of v2, /device:TPU:25, one launch (start us, length us, event | category | flops | bytes accessed | tf_op | source)
XLA Modules:
  0.0 140.2 jit_solution(10406405301753789609)
XLA Ops:
  0.0 106.6 %chain.1 = (f32[2,1280,256]{2,1,0:T(8,128)}, f32[2,256,2560]{2,1,0:T(8,128)}, f32[2,256,256]{2,1,0:T(8,128)}, f32[2,256,256]{2,1,0:T(8,128)}, f32[256,256]{1,0:T(8,128)}) custom-call(f32[1280,2560]{1,0:T(8,128)} %a_ref.3), custom_call_target="tpu_custom_call" | custom-call | tf_op jit(solution)/shard_map/chain/pallas_call | solution.py:366
  106.6 33.5 %update.1 = f32[1280,2560]{1,0:T(8,128)} custom-call(f32[1280,2560]{1,0:T(8,128)} %a_ref.3, f32[2,1280,256]{2,1,0:T(8,128)} %get-tuple-element.10.r_ref, f32[2,256,2560]{2,1,0:T(8,128)} %get-tuple-element.11.c_ref, f32[2,256,256]{2,1,0:T(8,128)} %get-tuple-element.12.v_ref, f32[2,256,256]{2,1,0:T(8,128)} %get-tuple-element.13.lt_ref, ...), custom_call_target="tpu_custom_call" | custom-call | tf_op jit(solution)/shard_map/update/pallas_call | solution.py:395

commit v3 on v2

--- a/solution.py
+++ b/solution.py
@@ -7,7 +7,8 @@
 from jax.sharding import PartitionSpec as P
 
 NB = 256
-BK = 32
+BK = 64
+STEPS = 2
 PIECES = 4
 MESH = pl.DeviceIdType.MESH
 HIGH = lax.Precision.HIGHEST
@@ -25,22 +26,32 @@
     sub = lax.broadcasted_iota(jnp.int32, (BK, 128), 0)
     w = jnp.where(lane < BK, lead, jnp.where(lane == sub + BK, 1.0, 0.0))
     scale = jnp.ones((BK, 128), jnp.float32)
-    for j in range(0, BK, 2):
-        c0 = jnp.broadcast_to(w[:, j:j + 1], (BK, 128))
-        c1 = jnp.broadcast_to(w[:, j + 1:j + 2], (BK, 128))
-        r0 = jnp.broadcast_to(w[j:j + 1, :], (BK, 128))
-        r1 = jnp.broadcast_to(w[j + 1:j + 2, :], (BK, 128))
-        d = jnp.broadcast_to(c0[j:j + 1, :], (BK, 128))
-        e = jnp.broadcast_to(c0[j + 1:j + 2, :], (BK, 128))
-        f = jnp.broadcast_to(c1[j + 1:j + 2, :], (BK, 128))
-        inv_d = 1.0 / d
-        inv_f = d / (f * d - e * e)
-        ratio = e * inv_d
-        m0 = jnp.where(sub > j, c0 * inv_d, 0.0)
-        r1n = r1 - ratio * r0
-        m1 = jnp.where(sub > j + 1, (c1 - ratio * c0) * inv_f, 0.0)
-        w = w - m0 * r0 - m1 * r1n
-        scale = jnp.where(sub == j, inv_d, jnp.where(sub == j + 1, inv_f, scale))
+    for j in range(0, BK, 4):
+        c = [jnp.broadcast_to(w[:, j + q:j + q + 1], (BK, 128)) for q in range(4)]
+        r = [w[j + q:j + q + 1, :] for q in range(4)]
+        ms, rs = [], []
+        for h in (0, 2):
+            c0, c1 = c[h], c[h + 1]
+            r0, r1 = r[h], r[h + 1]
+            i = j + h
+            d, e, f = c0[i:i + 1, :], c0[i + 1:i + 2, :], c1[i + 1:i + 2, :]
+            inv_d = 1.0 / d
+            inv_f = d / (f * d - e * e)
+            ratio = e * inv_d
+            m0 = jnp.where(sub > i, c0 * inv_d, 0.0)
+            m1 = jnp.where(sub > i + 1, (c1 - ratio * c0) * inv_f, 0.0)
+            r1 = r1 - ratio * r0
+            ms += [m0, m1]
+            rs += [r0, r1]
+            scale = jnp.where(sub == i, inv_d, jnp.where(sub == i + 1, inv_f, scale))
+            if h == 0:
+                for p in (2, 3):
+                    e0 = c[p][i:i + 1, :]
+                    e1 = c[p][i + 1:i + 2, :] - ratio * e0
+                    r[p] = r[p] - m0[j + p:j + p + 1, :] * r0 - m1[j + p:j + p + 1, :] * r1
+                    c[p] = c[p] - m0 * e0 - m1 * e1
+        for m, x in zip(ms, rs):
+            w = w - m * x
     w = w * jnp.sqrt(scale)
     vd = pltpu.roll(w, 128 - BK, 1)[:, :BK]
     new = dot(vd, rows)
@@ -196,33 +207,50 @@
 
         lax.fori_loop(0, chunks, step, 0)
 
+    def r_wait(k, c):
+        remote(r_piece(k, c), r_send.at[k, 0, c], r_recv.at[k, c], (row, col)).wait_recv()
+
+    def c_wait(k, c):
+        remote(c_piece(k, c), c_send.at[k, 0, c], c_recv.at[k, c], (row, col)).wait_recv()
+
+    def r_up(k, c):
+        r_sends(k, c)[0][1].start()
+
+    middle = (col >= 1) & (col < n_col - 1)
+
+    def r_early():
+        def step(c, carry):
+            r_wait(1, c)
+            r_up(1, c)
+            return carry
+
+        lax.fori_loop(0, early, step, 0)
+
     def pump(s, tiles=True):
         if tiles:
             for i in (1, 2):
                 pl.when((row != roots[i][0]) & (s == ring_hops[roots[i][0]]))(lambda i=i: d_relay(i))
+
+        def r_one(c):
+            r_wait(0, c)
+            r_up(0, c)
+
+            @pl.when(c < chunks - early)
+            def _():
+                pl.when(col > 1)(lambda: r_wait(1, c + early))
+                r_up(1, c + early)
+
+        u = s - col
+        pl.when(middle & (u >= 0) & (u < 2 * chunks) & (lax.rem(u + 2 * n_col, 2) == 0))(lambda: r_one(u // 2))
         for k in range(2):
-            far = jnp.where(col >= k, col - k, k - col)
-
-            def r_one(c, k=k):
-                pl.when(col != k)(remote(r_piece(k, c), r_send.at[k, 0, c], r_recv.at[k, c], (row, col)).wait_recv)
-                for cond, copy in r_sends(k, c):
-                    pl.when((col != k) & cond)(copy.start)
-                if k == 1:
-                    @pl.when((col == k) & (c < chunks - early))
-                    def _():
-                        cond, copy = r_sends(k, c + early)[0]
-                        pl.when(cond)(copy.start)
-
             def c_one(c, k=k):
-                remote(c_piece(k, c), c_send.at[k, 0, c], c_recv.at[k, c], (row, col)).wait_recv()
+                c_wait(k, c)
                 for cond, copy in c_sends(k, c):
                     pl.when(cond)(copy.start)
 
-            u = s - far
-            c = (5 * jnp.maximum(u, 0) + 6) // 7
-            pl.when((u >= 0) & ((7 * c) // 5 == u) & (c < chunks))(lambda: r_one(c))
-            hop = hops[k]
-            pl.when((s >= hop) & (s < hop + chunks) & (row != k))(lambda: c_one(s - hop))
+            u = s - hops[k]
+            pl.when((core == k) & (row != k) & (u >= 0) & (u < 2 * chunks) & (lax.rem(u + n_row, 2) == 0))(
+                lambda c_one=c_one, u=u: c_one(u // 2))
 
     pl.when(row > 1)(lambda: [r_root(k) for k in range(2)] and None)
     d_relay(0)
@@ -230,42 +258,55 @@
     pl.when(row <= 1)(lambda: [r_root(k) for k in range(2)] and None)
     for k in range(2):
         pl.when(row == k)(functools.partial(c_root, k))
+    pl.when(middle & (col > 1))(r_early)
 
     blocks = NB // BK
     set_work(work, dbuf[0])
 
     def first(s, carry):
-        pump(s)
+        for q in range(STEPS):
+            pump(s * STEPS + q)
         factor_block(work, lt_out.at[0], v_out.at[0], s)
         return carry
 
     lax.fori_loop(0, blocks, first, 0)
     most = half // 2 + 2
-    if most > blocks:
+    if most > blocks * STEPS:
         def tiles_rest(s, carry):
             for i in (1, 2):
                 pl.when((row != roots[i][0]) & (s == ring_hops[roots[i][0]]))(lambda i=i: d_relay(i))
             return carry
 
-        lax.fori_loop(blocks, most, tiles_rest, 0)
+        lax.fori_loop(blocks * STEPS, most, tiles_rest, 0)
     mid = dot(dbuf[1], v_out[0], ((1,), (1,)))
     mid_out[...] = mid
     set_work(work, dbuf[2] - dot(mid, mid, ((1,), (1,))))
 
     def second(s, carry):
-        pump(s + blocks, False)
+        for q in range(STEPS):
+            pump((s + blocks) * STEPS + q, False)
         factor_block(work, lt_out.at[1], v_out.at[1], s)
         return carry
 
     lax.fori_loop(0, blocks, second, 0)
 
-    total = max((7 * (chunks - 1)) // 5 + n_col, chunks + half)
-    if total > 2 * blocks:
+    total = 2 * chunks - 1 + max(n_col - 1, half)
+    done = 2 * blocks * STEPS
+    if total > done:
         def rest(s, carry):
             pump(s, False)
             return carry
 
-        lax.fori_loop(2 * blocks, total, rest, 0)
+        lax.fori_loop(done, total, rest, 0)
+
+    def ends(c, carry):
+        pl.when(col == n_col - 1)(lambda: r_wait(0, c))
+        pl.when((col == 0) | ((col == n_col - 1) & (col > 1)))(lambda: r_wait(1, c))
+        for k in range(2):
+            pl.when(core != k)(lambda k=k: c_wait(k, c))
+        return carry
+
+    lax.fori_loop(0, chunks, ends, 0)
 
     back = [local(rbuf, r_out, loc.at[0]), local(cbuf, c_out, loc.at[1])]
     for copy in back:

time: 140 us -> 121 us (0.86)
  Pallas kernels: 140 us -> 121 us
    pallas_call x1, Pallas kernels: 107 us -> 87.7 us  [body(): pl.pallas_call(functools.partial(chain_kernel, n_row, n_col, chunks), out...]
where the time goes in v3:
time: 121 us
  Pallas kernels  121 us (100%)
    pallas_call x1, Pallas kernels, body(): pl.pallas_call(functools.partial(chain_kernel, n_row, n_col, chunks), out...  87.7 us
    pallas_call x1, Pallas kernels, body(): pl.pallas_call(functools.partial(update_kernel, n_row, n_col), grid=(n_ro...  33.5 us

profile of v3, /device:TPU:25, one launch (start us, length us, event | category | flops | bytes accessed | tf_op | source)
XLA Modules:
  0.0 121.2 jit_solution(6256799723519168020)
XLA Ops:
  0.0 87.7 %chain.1 = (f32[2,1280,256]{2,1,0:T(8,128)}, f32[2,256,2560]{2,1,0:T(8,128)}, f32[2,256,256]{2,1,0:T(8,128)}, f32[2,256,256]{2,1,0:T(8,128)}, f32[256,256]{1,0:T(8,128)}) custom-call(f32[1280,2560]{1,0:T(8,128)} %a_ref.3), custom_call_target="tpu_custom_call" | custom-call | tf_op jit(solution)/shard_map/chain/pallas_call | solution.py:407
  87.7 33.5 %update.1 = f32[1280,2560]{1,0:T(8,128)} custom-call(f32[1280,2560]{1,0:T(8,128)} %a_ref.3, f32[2,1280,256]{2,1,0:T(8,128)} %get-tuple-element.10.r_ref, f32[2,256,2560]{2,1,0:T(8,128)} %get-tuple-element.11.c_ref, f32[2,256,256]{2,1,0:T(8,128)} %get-tuple-element.12.v_ref, f32[2,256,256]{2,1,0:T(8,128)} %get-tuple-element.13.lt_ref, ...), custom_call_target="tpu_custom_call" | custom-call | tf_op jit(solution)/shard_map/update/pallas_call | solution.py:436

commit v4 on v3

--- a/solution.py
+++ b/solution.py
@@ -80,7 +80,7 @@
 
 
 def chain_kernel(n_row, n_col, chunks, a_ref, r_out, c_out, v_out, lt_out, mid_out,
-                 rbuf, cbuf, dbuf, work, r_send, r_recv, c_send, c_recv, d_send, d_recv, loc):
+                 rbuf, cbuf, dbuf, work, r_send, r_recv, c_send, c_recv, d_send, d_recv, loc, right):
     row = lax.axis_index("row")
     col = lax.axis_index("col")
     n_rows = rbuf.shape[1]
@@ -253,12 +253,13 @@
                 lambda c_one=c_one, u=u: c_one(u // 2))
 
     pl.when(row > 1)(lambda: [r_root(k) for k in range(2)] and None)
+    pl.when((row > 1) & middle & (col > 1))(r_early)
     d_relay(0)
     pl.when(row == 1)(lambda: [d_relay(i) for i in (1, 2)] and None)
     pl.when(row <= 1)(lambda: [r_root(k) for k in range(2)] and None)
     for k in range(2):
         pl.when(row == k)(functools.partial(c_root, k))
-    pl.when(middle & (col > 1))(r_early)
+    pl.when((row <= 1) & middle & (col > 1))(r_early)
 
     blocks = NB // BK
     set_work(work, dbuf[0])
@@ -292,25 +293,46 @@
 
     total = 2 * chunks - 1 + max(n_col - 1, half)
     done = 2 * blocks * STEPS
-    if total > done:
-        def rest(s, carry):
-            pump(s, False)
-            return carry
-
-        lax.fori_loop(done, total, rest, 0)
+    ahead = max(done, total - chunks) if chunks - 1 + half > done else done
+
+    def rest(s, carry):
+        pump(s, False)
+        return carry
+
+    if ahead > done:
+        lax.fori_loop(done, ahead, rest, 0)
+
+    def panels(c, carry):
+        pump(ahead + c, False)
+        for k in range(2):
+            pl.when(core != k)(lambda k=k: c_wait(k, c))
+        span = pl.ds(pl.multiple_of(c * c_step, c_step), c_step)
+        p0 = halves(dot3(halves(v_out[0]), halves(cbuf[0, :, span])))
+        left = cbuf[1, :, span] - dot3(halves(mid_out[...]), p0)
+        p1 = halves(dot3(halves(v_out[1]), halves(left)))
+        for k, (hi, lo) in enumerate((p0, p1)):
+            right[pl.ds(3 * k * NB, NB), span] = hi
+            right[pl.ds((3 * k + 1) * NB, NB), span] = lo
+            right[pl.ds((3 * k + 2) * NB, NB), span] = hi
+        return carry
+
+    lax.fori_loop(0, chunks, panels, 0)
+    if total > ahead + chunks:
+        lax.fori_loop(ahead + chunks, total, rest, 0)
+    c_back = local(right, c_out, loc.at[1])
+    c_back.start()
 
     def ends(c, carry):
         pl.when(col == n_col - 1)(lambda: r_wait(0, c))
         pl.when((col == 0) | ((col == n_col - 1) & (col > 1)))(lambda: r_wait(1, c))
-        for k in range(2):
-            pl.when(core != k)(lambda k=k: c_wait(k, c))
         return carry
 
     lax.fori_loop(0, chunks, ends, 0)
 
-    back = [local(rbuf, r_out, loc.at[0]), local(cbuf, c_out, loc.at[1])]
+    back = [local(rbuf, r_out, loc.at[0])]
     for copy in back:
         copy.start()
+    back.append(c_back)
 
     def d_drain(p, carry):
         for i in range(3):
@@ -342,24 +364,11 @@
     return part(a[0], b[0]) + (part(a[0], b[1]) + part(a[1], b[0]))
 
 
-def update_kernel(n_row, n_col, a_ref, r_ref, c_ref, v_ref, lt_ref, mid_ref, o_ref, right):
+def update_kernel(n_row, n_col, a_ref, r_ref, right, v_ref, lt_ref, mid_ref, o_ref):
     t = pl.program_id(0)
     row = lax.axis_index("row")
     col = lax.axis_index("col")
     n_cols = a_ref.shape[1]
-
-    @pl.when(t == 0)
-    def _():
-        @pl.loop(0, n_cols // NB)
-        def _(s):
-            span = pl.ds(pl.multiple_of(s * NB, NB), NB)
-            p0 = halves(dot3(halves(v_ref[0]), halves(c_ref[0, :, span])))
-            rest = c_ref[1, :, span] - dot3(halves(mid_ref[...]), p0)
-            p1 = halves(dot3(halves(v_ref[1]), halves(rest)))
-            for k, (hi, lo) in enumerate((p0, p1)):
-                right[pl.ds(3 * k * NB, NB), span] = hi
-                right[pl.ds((3 * k + 1) * NB, NB), span] = lo
-                right[pl.ds((3 * k + 2) * NB, NB), span] = hi
 
     g = t * n_row + row
     across = ((1,), (1,))
@@ -408,7 +417,7 @@
         functools.partial(chain_kernel, n_row, n_col, chunks),
         out_shape=(
             jax.ShapeDtypeStruct((2, n_rows, NB), f32),
-            jax.ShapeDtypeStruct((2, NB, n_cols), f32),
+            jax.ShapeDtypeStruct((6 * NB, n_cols), jnp.bfloat16),
             jax.ShapeDtypeStruct((2, NB, NB), f32),
             jax.ShapeDtypeStruct((2, NB, NB), f32),
             jax.ShapeDtypeStruct((NB, NB), f32),
@@ -427,6 +436,7 @@
             pltpu.SemaphoreType.DMA((3, 5, PIECES)),
             pltpu.SemaphoreType.DMA((3, PIECES)),
             pltpu.SemaphoreType.DMA((7,)),
+            pltpu.VMEM((6 * NB, n_cols), jnp.bfloat16),
         ],
         compiler_params=pltpu.CompilerParams(
             collective_id=0, has_side_effects=True, vmem_limit_bytes=60 * 2**20),
@@ -440,13 +450,12 @@
         in_specs=[
             pl.BlockSpec((NB, n_cols), lambda t: (t, 0)),
             pl.BlockSpec((2, NB, NB), lambda t: (0, t, 0)),
-            whole((2, NB, n_cols)),
+            whole((6 * NB, n_cols)),
             whole((2, NB, NB)),
             whole((2, NB, NB)),
             whole((NB, NB)),
         ],
         out_specs=pl.BlockSpec((NB, n_cols), lambda t: (t, 0)),
-        scratch_shapes=[pltpu.VMEM((6 * NB, n_cols), jnp.bfloat16)],
         compiler_params=pltpu.CompilerParams(vmem_limit_bytes=60 * 2**20),
         name="update",
     )(matrix, r, c, v, lt, mid)

time: 121 us -> 118 us (0.975)
  the two profiles are of different devices: /device:TPU:25 before, /device:TPU:17 now
where the time goes in v4:
time: 118 us
  Pallas kernels  118 us (100%)
    pallas_call x1, Pallas kernels, body(): pl.pallas_call(functools.partial(chain_kernel, n_row, n_col, chunks), out...  93 us
    pallas_call x1, Pallas kernels, body(): pl.pallas_call(functools.partial(update_kernel, n_row, n_col), grid=(n_ro...  24.9 us

profile of v4, /device:TPU:17, one launch (start us, length us, event | category | flops | bytes accessed | tf_op | source)
XLA Modules:
  0.0 118.0 jit_solution(17087055770461169050)
XLA Ops:
  0.0 93.0 %chain.1 = (f32[2,1280,256]{2,1,0:T(8,128)}, bf16[1536,2560]{1,0:T(8,128)(2,1)}, f32[2,256,256]{2,1,0:T(8,128)}, f32[2,256,256]{2,1,0:T(8,128)}, f32[256,256]{1,0:T(8,128)}) custom-call(f32[1280,2560]{1,0:T(8,128)} %a_ref.3), custom_call_target="tpu_custom_call" | custom-call | tf_op jit(solution)/shard_map/chain/pallas_call | solution.py:416
  93.0 24.9 %update.1 = f32[1280,2560]{1,0:T(8,128)} custom-call(f32[1280,2560]{1,0:T(8,128)} %a_ref.3, f32[2,1280,256]{2,1,0:T(8,128)} %get-tuple-element.10.r_ref, bf16[1536,2560]{1,0:T(8,128)(2,1)} %get-tuple-element.11.right, f32[2,256,256]{2,1,0:T(8,128)} %get-tuple-element.12.v_ref, f32[2,256,256]{2,1,0:T(8,128)} %get-tuple-element.13.lt_ref, ...), custom_call_target="tpu_custom_call" | custom-call | tf_op jit(solution)/shard_map/update/pallas_call | solution.py:446

commit v5 on v4

--- a/solution.py
+++ b/solution.py
@@ -171,12 +171,15 @@
     def c_piece(k, c):
         return cbuf.at[k, :, pl.ds(pl.multiple_of(c * c_step, c_step), c_step)]
 
+    def keep(c):
+        return (row > 1) | (c >= NB // r_step)
+
     def r_sends(k, c):
         piece = r_piece(k, c)
         return (
-            ((col >= k) & (col < n_col - 1),
+            ((col >= k) & (col < n_col - 1) & keep(c),
              remote(piece, r_send.at[k, 0, c], r_recv.at[k, c], (row, jnp.minimum(col + 1, n_col - 1)))),
-            ((col <= k) & (col > 0),
+            ((col <= k) & (col > 0) & keep(c),
              remote(piece, r_send.at[k, 1, c], r_recv.at[k, c], (row, jnp.maximum(col - 1, 0)))),
         )
 
@@ -208,13 +211,13 @@
         lax.fori_loop(0, chunks, step, 0)
 
     def r_wait(k, c):
-        remote(r_piece(k, c), r_send.at[k, 0, c], r_recv.at[k, c], (row, col)).wait_recv()
+        pl.when(keep(c))(remote(r_piece(k, c), r_send.at[k, 0, c], r_recv.at[k, c], (row, col)).wait_recv)
 
     def c_wait(k, c):
         remote(c_piece(k, c), c_send.at[k, 0, c], c_recv.at[k, c], (row, col)).wait_recv()
 
     def r_up(k, c):
-        r_sends(k, c)[0][1].start()
+        pl.when(keep(c))(r_sends(k, c)[0][1].start)
 
     middle = (col >= 1) & (col < n_col - 1)
 

time: 118 us -> 110 us (0.932)
  the two profiles are of different devices: /device:TPU:17 before, /device:TPU:20 now
where the time goes in v5:
time: 110 us
  Pallas kernels  110 us (100%)
    pallas_call x1, Pallas kernels, body(): pl.pallas_call(functools.partial(chain_kernel, n_row, n_col, chunks), out...  85.3 us
    pallas_call x1, Pallas kernels, body(): pl.pallas_call(functools.partial(update_kernel, n_row, n_col), grid=(n_ro...  24.8 us

profile of v5, /device:TPU:20, one launch (start us, length us, event | category | flops | bytes accessed | tf_op | source)
XLA Modules:
  0.0 110.1 jit_solution(3569748298572613933)
XLA Ops:
  0.0 85.3 %chain.1 = (f32[2,1280,256]{2,1,0:T(8,128)}, bf16[1536,2560]{1,0:T(8,128)(2,1)}, f32[2,256,256]{2,1,0:T(8,128)}, f32[2,256,256]{2,1,0:T(8,128)}, f32[256,256]{1,0:T(8,128)}) custom-call(f32[1280,2560]{1,0:T(8,128)} %a_ref.3), custom_call_target="tpu_custom_call" | custom-call | tf_op jit(solution)/shard_map/chain/pallas_call | solution.py:419
  85.3 24.8 %update.1 = f32[1280,2560]{1,0:T(8,128)} custom-call(f32[1280,2560]{1,0:T(8,128)} %a_ref.3, f32[2,1280,256]{2,1,0:T(8,128)} %get-tuple-element.10.r_ref, bf16[1536,2560]{1,0:T(8,128)(2,1)} %get-tuple-element.11.right, f32[2,256,256]{2,1,0:T(8,128)} %get-tuple-element.12.v_ref, f32[2,256,256]{2,1,0:T(8,128)} %get-tuple-element.13.lt_ref, ...), custom_call_target="tpu_custom_call" | custom-call | tf_op jit(solution)/shard_map/update/pallas_call | solution.py:449
